TPU v7x, 256 devices: a whole 4x4x8 slice. The times are simulated.
256 devices in a mesh: dp: 8 (over y, z_hi), expert: 32 (over z_lo, x, core).
Axes of the slice: x: 4, y: 4, z: 8 (z_hi: 2, z_lo: 4; z = z_hi * 4 + z_lo), core: 2. Of those that a mesh axis runs over, the one named last changes fastest.
Arguments:
- activations: bfloat16 [32768, 4096], P(('dp', 'expert')), may hold values from -6 to 6
- cotangent: bfloat16 [32768, 4096], P(('dp', 'expert')), may hold values from -6 to 6
- expert_ids: int32 [32768, 1], P(('dp', 'expert')), may hold values from 0 to 127; in each aligned block of 128 rows (0 to 127, 128 to 255, ...) at most 2 rows name the same one
- gate_probs: float32 [32768, 1], P(('dp', 'expert')), may hold values from 0.2 to 1
- gate_up: bfloat16 [32, 2, 4096, 1536], P('expert', None, None, 'dp'), may hold values from -0.09375 to 0.09375
- down_proj: bfloat16 [32, 1536, 4096], P('expert', 'dp'), may hold values from -0.15625 to 0.15625
Outputs:
- input_grad: bfloat16 [32768, 4096], P(('dp', 'expert'))
- grad_gate_up: bfloat16 [32, 2, 4096, 1536], P('expert', None, None, 'dp')
- grad_down: bfloat16 [32, 1536, 4096], P('expert', 'dp')
Inputs may be any that keep to these rules, and one draw needn't show every extreme that they name: `expert_ids`: expert e < 32 is held by index e of the expert axis. Among the 128 tokens of one device no expert is named more than 2 times, a bound that some block reaches.
All inputs are finite; a program needn't handle non-finite values.
Results may differ from a plain program's by a relative error of at most 0.0058.
Values may be sent and summed in bfloat16 or wider, within the bound.
A program may use at most 128 MiB of HBM per device.

v0:
```python
import jax
import jax.numpy as jnp
from jax import lax
from jax.sharding import PartitionSpec as P

CAP = 2


def contract(left, right, left_dim, right_dim):
    return lax.dot_general(
        left, right, (((left_dim,), (right_dim,)), ((), ())), preferred_element_type=jnp.float32
    )


def block_backward(rows_tok, rows_cot, pair_weights, down_weights):
    pre_gate = jnp.dot(rows_tok, pair_weights[0], preferred_element_type=jnp.float32)
    pre_up = jnp.dot(rows_tok, pair_weights[1], preferred_element_type=jnp.float32)
    sigmoid_gate = jax.nn.sigmoid(pre_gate)
    activated = pre_gate * sigmoid_gate
    hidden = (activated * pre_up).astype(jnp.bfloat16)
    hidden_grad = contract(rows_cot, down_weights, 1, 1)
    gate_grad = (
        hidden_grad * pre_up * sigmoid_gate * (1.0 + pre_gate * (1.0 - sigmoid_gate))
    ).astype(jnp.bfloat16)
    up_grad = (hidden_grad * activated).astype(jnp.bfloat16)
    total_down = contract(hidden, rows_cot, 0, 0)
    total_gate = contract(rows_tok, gate_grad, 0, 0)
    total_up = contract(rows_tok, up_grad, 0, 0)
    input_rows = contract(gate_grad, pair_weights[0], 1, 1) + contract(
        up_grad, pair_weights[1], 1, 1
    )
    return (total_gate, total_up, total_down, input_rows)


def expert_rows(rows_tok, rows_cot, pair_weights, down_weights):
    row_count = rows_tok.shape[0]
    block_rows = min(256, row_count)
    model_width = rows_tok.shape[1]
    unit_count = down_weights.shape[0]
    alive_flag = jnp.any(rows_cot != 0, axis=1).astype(jnp.int32)
    ordering = jnp.argsort(1 - alive_flag, stable=True)
    live_count = jnp.sum(alive_flag)
    block_count = (live_count + block_rows - 1) // block_rows

    def advance(counter, carry_state):
        total_gate, total_up, total_down, input_all = carry_state
        picked = lax.dynamic_slice_in_dim(ordering, counter * block_rows, block_rows)
        part_tok = jnp.take(rows_tok, picked, axis=0)
        part_cot = jnp.take(rows_cot, picked, axis=0)
        more_gate, more_up, more_down, input_rows = block_backward(
            part_tok, part_cot, pair_weights, down_weights
        )
        input_all = input_all.at[picked].set(input_rows)
        return (total_gate + more_gate, total_up + more_up, total_down + more_down, input_all)

    initial = (
        jnp.zeros((model_width, unit_count), jnp.float32),
        jnp.zeros((model_width, unit_count), jnp.float32),
        jnp.zeros((unit_count, model_width), jnp.float32),
        jnp.zeros((row_count, model_width), jnp.float32),
    )
    total_gate, total_up, total_down, input_all = lax.fori_loop(0, block_count, advance, initial)
    return (jnp.stack([total_gate, total_up]), total_down, input_all)


def per_device(activations, cotangent, expert_ids, gate_probs, gate_up, down_proj):
    experts = lax.axis_size("expert")
    identity = expert_ids[:, 0]
    in_window = identity < experts
    onehot = (identity[:, None] == jnp.arange(experts, dtype=jnp.int32)[None, :]).astype(jnp.int32)
    before = jnp.cumsum(onehot, axis=0) - onehot
    ranking = jnp.sum(before * onehot, axis=1)
    slot_index = identity * CAP + ranking
    slot_index = jnp.where(in_window, slot_index, -1)
    placing = (slot_index[None, :] == jnp.arange(experts * CAP, dtype=jnp.int32)[:, None]).astype(
        jnp.bfloat16
    )
    scaled = (gate_probs * cotangent.astype(jnp.float32)).astype(jnp.bfloat16)
    send_tok = jnp.dot(placing, activations, preferred_element_type=jnp.float32).astype(
        jnp.bfloat16
    )
    send_cot = jnp.dot(placing, scaled, preferred_element_type=jnp.float32).astype(jnp.bfloat16)
    got_tok, got_cot = (
        lax.all_to_all(send_tok, "expert", split_axis=0, concat_axis=0, tiled=True),
        lax.all_to_all(send_cot, "expert", split_axis=0, concat_axis=0, tiled=True),
    )
    all_tok, all_cot = (
        lax.all_gather(got_tok, "dp", axis=0, tiled=True),
        lax.all_gather(got_cot, "dp", axis=0, tiled=True),
    )
    own_pair = gate_up[0]
    own_down = down_proj[0]
    pair_total, down_total, partial_value = expert_rows(all_tok, all_cot, own_pair, own_down)
    summed = lax.psum_scatter(partial_value, "dp", scatter_dimension=0, tiled=True)
    rounded = summed.astype(jnp.bfloat16)
    returned = lax.all_to_all(rounded, "expert", split_axis=0, concat_axis=0, tiled=True)
    input_grad = contract(placing, returned, 0, 0).astype(jnp.bfloat16)
    return (
        input_grad,
        pair_total[None].astype(jnp.bfloat16),
        down_total[None].astype(jnp.bfloat16),
    )


def solution(mesh):
    in_specs = (
        P(("dp", "expert"), None),
        P(("dp", "expert"), None),
        P(("dp", "expert"), None),
        P(("dp", "expert"), None),
        P("expert", None, None, "dp"),
        P("expert", "dp", None),
    )
    out_specs = (P(("dp", "expert"), None), P("expert", None, None, "dp"), P("expert", "dp", None))
    return jax.shard_map(
        per_device, mesh=mesh, in_specs=in_specs, out_specs=out_specs, check_vma=False
    )
```

profile of v0, /device:TPU:1, one launch (start us, length us, event | category | flops | bytes accessed | tf_op | source)
XLA Modules:
  0.0 564.4 jit_solution(4953973455181101589)
XLA Ops:
  7.2 0.8 fusion.18
  8.0 0.2 reduce_window_sum.11
  8.2 0.8 select_reduce_fusion
  9.1 0.7 compare_select_fusion.1
  9.7 1.6 convolution_convert_fusion.2
  11.4 0.3 all_to_all.24
  11.7 26.2 %all_to_all.36 = bf16[32,2,4096]{2,1,0:T(2,128)(2,1)S(1)} all-to-all(bf16[32,2,4096]{2,1,0:T(2,128)(2,1)S(1)} %all_to_all.24), channel_id=1, replica_groups=mesh['dp'=8,'expert'=32] {'expert'}, dimensions={0} | all-to-all | bytes 1048576 | tf_op jit(solution)/shard_map/all_to_all | solution.py:85
  37.9 1.0 all_to_all.26
  39.0 0.3 convolution_convert_fusion.1
  39.3 0.3 all_to_all.27
  39.7 31.5 %all_to_all.37 = bf16[32,2,4096]{2,1,0:T(2,128)(2,1)S(1)} all-to-all(bf16[32,2,4096]{2,1,0:T(2,128)(2,1)S(1)} %all_to_all.27), channel_id=1, replica_groups=mesh['dp'=8,'expert'=32] {'expert'}, dimensions={0} | all-to-all | bytes 1048576 | tf_op jit(solution)/shard_map/all_to_all | solution.py:84
  71.2 1.0 all_to_all.29
  72.3 6.1 %copy.9 = bf16[1,2,4096,192]{3,2,1,0:T(8,128)(2,1)} copy(bf16[1,2,4096,192]{2,3,1,0:T(8,128)(2,1)} %param.14) | data formatting | bytes 6291456 | tf_op args[4]
  78.3 68.2 %all-gather.3.cloned.1.call-done = bf16[512,4096]{1,0:T(8,128)(2,1)} async-done(((bf16[64,4096]{1,0:T(8,128)(2,1)}), bf16[512,4096]{1,0:T(8,128)(2,1)}) %all-gather.3.cloned.1.call-update) | async-done | bytes 4194320 | tf_op jit(solution)/shard_map/all_gather | solution.py:89
  146.5 3.3 compare_reduce_fusion
  149.9 0.6 convert_subtract_fusion
  151.2 3.8 sort.17
  154.9 96.6 %all-gather.5.cloned.1.call-done = bf16[512,4096]{1,0:T(8,128)(2,1)} async-done(((bf16[64,4096]{1,0:T(8,128)(2,1)}), bf16[512,4096]{1,0:T(8,128)(2,1)}) %all-gather.5.cloned.1.call-update) | async-done | bytes 4194320 | tf_op jit(solution)/shard_map/all_gather | solution.py:88
  251.5 2.1 broadcast.32.clone
  253.6 2.1 broadcast_in_dim.28
  255.7 2.0 broadcast.32
  257.7 4.2 broadcast_in_dim.29
  262.0 46.4 %while.16 = (s32[]{:T(128)}, f32[4096,192]{0,1:T(8,128)}, f32[4096,192]{0,1:T(8,128)}, f32[192,4096]{1,0:T(8,128)}, f32[512,4096]{1,0:T(8,128)}, /*index=5*/s32[...) while((s32[]{:T(128)}, f32[4096,192]{0,1:T(8,128)}, ...), condition=%wide.region_7.9_spmd, body=%wide.region_5.8_spmd.sunk | while | flops 3231861248 | bytes 160641424 | solution.py:62
  262.0 0.1 compare_and_fusion.2
  262.1 6.6 %gather_fusion = bf16[256,4096]{1,0:T(8,128)(2,1)S(1)} fusion(bf16[512,4096]{1,0:T(8,128)(2,1)} %get-tuple-element.214, s32[1024]{0:T(1024)S(1)} %pad_clamp_fusion.2), kind=kCustom, calls=%fused_computation.clone.clone.1 | custom fusion | bytes 4195328 | tf_op jit(solution)/shard_map/while/body/jit(_take)/gather | solution.py:48
  268.7 2.8 fusion.51
  271.5 1.1 fusion.50
  272.6 7.9 %gather_fusion.1 = bf16[256,4096]{1,0:T(8,128)(2,1)} fusion(bf16[512,4096]{1,0:T(8,128)(2,1)} %get-tuple-element.215, s32[1024]{0:T(1024)S(1)} %pad_clamp_fusion.2), kind=kCustom, calls=%fused_computation.1.clone.clone.1 | custom fusion | bytes 4195328 | tf_op jit(solution)/shard_map/while/body/jit(_take)/gather | solution.py:49
  280.6 3.1 multiply_convert_fusion.9
  283.7 4.5 convolution_add_fusion.10
  288.2 0.9 convolution_add_fusion.8
  289.1 1.7 copy-done.5
  290.8 0.9 convolution_add_fusion.9
  291.7 1.7 copy-done.3
  293.5 0.3 copy-done.7
  293.8 0.8 fusion.52
  294.6 2.7 convolution_add_fusion.11
  297.3 11.1 %scatter_fusion = f32[512,4096]{1,0:T(8,128)} fusion(f32[512,4096]{1,0:T(8,128)} %get-tuple-element.196, s32[256]{0:T(256)S(1)} %get-tuple-element.173, f32[256,4096]{1,0:T(8,128)} %convolution_add_fusion.11), kind=kCustom, calls=%fused_computation.2.clone.1 | custom fusion | bytes 12583936 | tf_op jit(solution)/shard_map/while/body/scatter | solution.py:53
  308.4 4.4 convert_bitcast_fusion.1
  312.9 216.4 %reduce-scatter.2.cloned.1.call-done = f32[64,4096]{1,0:T(8,128)} async-done(((f32[512,4096]{1,0:T(8,128)}), f32[64,4096]{1,0:T(8,128)}) %reduce-scatter.2.cloned.1.call-update) | async-done | bytes 1048592 | tf_op jit(solution)/shard_map/reduce_scatter | solution.py:94
  529.3 1.3 convert_element_type.55
  530.5 1.1 all_to_all.30
  531.7 8.1 %all-to-all-start.2 = ((bf16[32,2,4096]{2,1,0:T(2,128)(2,1)}), bf16[32,2,4096]{2,1,0:T(2,128)(2,1)S(1)}, u32[]{:S(2)}, u32[]{:S(2)}) async-start(bf16[32,2,4096]{2,1,0:T(2,128)(2,1)} %all_to_all.30), calls=%async_computation.3 | async-start | bytes 1048576 | tf_op jit(solution)/shard_map/all_to_all | solution.py:96
  539.8 3.4 pad_maximum_fusion
  543.2 3.2 convert_bitcast_fusion
  546.4 9.8 %all-to-all-done.2 = bf16[32,2,4096]{2,1,0:T(2,128)(2,1)S(1)} async-done(((bf16[32,2,4096]{2,1,0:T(2,128)(2,1)}), bf16[32,2,4096]{2,1,0:T(2,128)(2,1)S(1)}, u32[]{:S(2)}, u32[]{:S(2)}) %all-to-all-start.2) | async-done | bytes 524320 | tf_op jit(solution)/shard_map/all_to_all | solution.py:96
  556.2 0.2 all_to_all.32
  556.5 1.5 convolution_convert_fusion
  (25 shorter events, 0.2 us)
Async XLA Ops:
  7.2 31.8 %copy-start = (bf16[128,4096]{1,0:T(8,128)(2,1)S(1)}, bf16[128,4096]{1,0:T(8,128)(2,1)}, u32[]{:S(2)}) copy-start(bf16[128,4096]{1,0:T(8,128)(2,1)} %param.10) | copy-start | bytes 3145732
  7.2 139.4 %all-gather.3.cloned.1.call-start = ((), (), s32[]{:S(2)}) async-start(), calls=%async_computation.4 | async-start | bytes 4718592 | tf_op jit(solution)/shard_map/all_gather | solution.py:89
  9.7 29.6 %copy-start.8 = (s32[128]{0:T(128)}, s32[128]{0:T(128)S(1)}, u32[]{:S(2)}) copy-start(s32[128]{0:T(128)S(1)} %compare_select_fusion.1) | copy-start | bytes 1540
  38.9 212.6 %all-gather.5.cloned.1.call-start = ((), (), s32[]{:S(2)}) async-start(), calls=%async_computation.5 | async-start | bytes 4718592 | tf_op jit(solution)/shard_map/all_gather | solution.py:88
  72.2 457.0 %reduce-scatter.2.cloned.1.call-start = ((), (), s32[]{:S(2)}) async-start(), calls=%async_computation.6 | async-start | bytes 9437184 | tf_op jit(solution)/shard_map/reduce_scatter | solution.py:94
  268.7 2.8 copy-start.6
  280.6 3.1 copy-start.1
  283.7 4.5 copy-start.4
  288.2 2.6 copy-start.2
  289.1 1.7 copy-start.5
  290.8 3.0 copy-start.7
  291.7 1.8 copy-start.3
  531.7 24.6 %all-to-all-start.2 = ((bf16[32,2,4096]{2,1,0:T(2,128)(2,1)}), bf16[32,2,4096]{2,1,0:T(2,128)(2,1)S(1)}, u32[]{:S(2)}, u32[]{:S(2)}) async-start(bf16[32,2,4096]{2,1,0:T(2,128)(2,1)} %all_to_all.30), calls=%async_computation.3 | async-start | bytes 1048576 | tf_op jit(solution)/shard_map/all_to_all | solution.py:96
  543.2 13.3 %copy-start.9 = (s32[128]{0:T(128)S(1)}, s32[128]{0:T(128)}, u32[]{:S(2)}) copy-start(s32[128]{0:T(128)} %copy-done.8) | copy-start | bytes 1540
Sparse Core Ops, SparseCore 0:
  39.1 107.4 all-gather.2
  149.7 101.7 all-gather.4
  308.5 220.6 reduce-scatter.1
where the time goes:
time: 566 us; the launch traced here: 564 us
  waiting for transfers between devices  391 us (69%)
  blocking collectives  57.8 us (10%)
  local copies, waits for them, and re-layouts  49.9 us (9%)
  other arithmetic  22.6 us (4%)
  matrix products  20.2 us (4%)
  between operations  14.5 us (3%)
  starting transfers between devices  8.24 us (1%)
    reduce_scatter x1, waiting for transfers between devices, per_device(): lax.psum_scatter(partial_value, 'dp', scatter_dimension=0, tiled=True)  216 us
    all_gather x1, waiting for transfers between devices, per_device(): lax.all_gather(got_tok, 'dp', axis=0, tiled=True)  96.6 us
    all_gather x1, waiting for transfers between devices, per_device(): lax.all_gather(got_cot, 'dp', axis=0, tiled=True)  68.2 us
    all_to_all x1, blocking collectives, per_device(): lax.all_to_all(send_tok, 'expert', split_axis=0, concat_axis=0, tiled=True)  31.5 us
    all_to_all x1, blocking collectives, per_device(): lax.all_to_all(send_cot, 'expert', split_axis=0, concat_axis=0, tiled=True)  26.2 us
    dot_general x7, matrix products, contract(): lax.dot_general(left, right, (((left_dim,), (right_dim,)), ((), ())), pre...  14.4 us
  transfers between devices with their start and end apart: 4, of which 4 were waited for; matrix products, arithmetic and copies ran while one was open for 4% of the time, Pallas kernels for 0%

commit v1 on v0

v1 whole, which is shorter than its diff:
```python
import jax
import jax.numpy as jnp
from jax import lax
from jax.experimental import pallas as pl
from jax.experimental.pallas import tpu as pltpu
from jax.sharding import PartitionSpec as P

CAP = 2
MESH = pl.DeviceIdType.MESH
F32 = jnp.float32
BF16 = jnp.bfloat16

NY = 4
NZH = 2
NZL = 4
NZ = NZH * NZL
NXC = 8
SLAB = NXC * CAP
OFFSETS = (0, 1, 7, 2, 6, 3, 5, 4)
CHUNK = 512


def nt(left, right):
    return lax.dot_general(left, right, (((1,), (1,)), ((), ())), preferred_element_type=F32)


def nn(left, right):
    return lax.dot_general(left, right, (((1,), (0,)), ((), ())), preferred_element_type=F32)


def tn(left, right):
    return lax.dot_general(left, right, (((0,), (0,)), ((), ())), preferred_element_type=F32)


def kernel(
    ids_ref,
    probs_ref,
    act_hbm,
    cot_hbm,
    pair_hbm,
    down_hbm,
    out_hbm,
    gpair_hbm,
    gdown_hbm,
    act,
    cot,
    pair,
    down,
    send,
    recv1,
    perm,
    rows,
    accs,
    gate_t,
    up_t,
    hid_t,
    own,
    part,
    relayed,
    from_up,
    from_down,
    summed,
    back,
    xsend,
    final,
    outv,
    gpair,
    gdown,
    load_sem,
    store_sem,
    x_send,
    x_recv,
    z_send,
    z_recv,
    y_send,
    y_recv,
    f_send,
    f_recv,
    rl_send,
    rl_recv,
    ru_send,
    ru_recv,
    rd_send,
    rd_recv,
    rz_send,
    rz_recv,
    rx_send,
    rx_recv,
):
    width = act.shape[1]
    chunks = width // CHUNK
    tokens = act.shape[0]
    e = lax.axis_index("expert")
    d = lax.axis_index("dp")
    zl = lax.div(e, NXC)
    xc = lax.rem(e, NXC)
    y = lax.div(d, NZH)
    z = lax.rem(d, NZH) * NZL + zl

    def dev(yy, zz, xx):
        return (yy * NZH + lax.div(zz, NZL), lax.rem(zz, NZL) * NXC + xx)

    def at_x(i):
        return dev(y, z, lax.rem(xc + i, NXC))

    def at_z(i):
        return dev(y, lax.rem(z + i, NZ), xc)

    up = dev(lax.rem(y + 1, NY), z, xc)
    dn = dev(lax.rem(y + NY - 1, NY), z, xc)

    def cols(c):
        return pl.ds(pl.multiple_of(c * CHUNK, CHUNK), CHUNK)

    def remote(src, dst, ssem, rsem, where):
        return pltpu.make_async_remote_copy(
            src_ref=src, dst_ref=dst, send_sem=ssem, recv_sem=rsem, device_id=where, device_id_type=MESH
        )

    loads = [
        pltpu.make_async_copy(act_hbm, act, load_sem.at[0]),
        pltpu.make_async_copy(cot_hbm, cot, load_sem.at[1]),
        pltpu.make_async_copy(pair_hbm, pair, load_sem.at[2]),
        pltpu.make_async_copy(down_hbm, down, load_sem.at[3]),
    ]
    for copy in loads:
        copy.start()
    barrier = pltpu.get_barrier_semaphore()
    partners = [at_x(i) for i in range(1, NXC)] + [at_z(i) for i in range(1, NZ)] + [up, dn]
    for partner in partners:
        pl.semaphore_signal(barrier, inc=1, device_id=partner, device_id_type=MESH)

    ids = ids_ref[...]
    ids_wide = jnp.broadcast_to(ids.astype(F32), (tokens, tokens))
    ids_tall = ids_wide.T
    row_at = lax.broadcasted_iota(jnp.int32, (tokens, tokens), 0)
    col_at = lax.broadcasted_iota(jnp.int32, (tokens, tokens), 1)
    earlier = jnp.where((ids_wide == ids_tall) & (row_at < col_at), 1.0, 0.0)
    rank = jnp.sum(earlier, axis=0, keepdims=True).astype(jnp.int32)
    offset = lax.rem(lax.div(ids, NXC) + NZL - zl, NZL)
    inside = ids < NZL * NXC
    place = lax.rem(ids, NXC) * (2 * NZL * CAP) + offset * CAP + rank
    place = jnp.where(inside, place, -1024)
    pick_tok = jnp.where(row_at == place, 1.0, 0.0).astype(BF16)
    pick_cot = jnp.where(row_at == place + NZL * CAP, 1.0, 0.0).astype(BF16)
    slot = lax.rem(ids, NXC) * (NZL * CAP) + offset * CAP + rank
    slot = jnp.where(inside, slot, -1024)
    half_row = lax.broadcasted_iota(jnp.int32, (NXC * NZL * CAP, tokens), 0)
    pick_out = jnp.where(half_row == slot, 1.0, 0.0).astype(BF16)

    loads[0].wait()
    loads[1].wait()
    probs = probs_ref[...]

    def gather_rows(c, carry):
        scaled = (probs * cot[:, cols(c)].astype(F32)).astype(BF16)
        got = nn(pick_tok, act[:, cols(c)]) + nn(pick_cot, scaled)
        got = got.astype(BF16).reshape(NXC, 2 * NZL * CAP, CHUNK)
        send[:, :, cols(c)] = got
        return carry

    lax.fori_loop(0, chunks, gather_rows, 0)
    pl.semaphore_wait(barrier, len(partners))

    x_copies = []
    for i in range(1, NXC):
        copy = remote(
            send.at[lax.rem(xc + i, NXC)], recv1.at[i], x_send.at[i], x_recv.at[i], at_x(i)
        )
        copy.start()
        x_copies.append(copy)
    own_copy = pltpu.make_async_copy(send.at[xc], recv1.at[0], load_sem.at[4])
    own_copy.start()
    for copy in x_copies:
        copy.wait_recv()
    own_copy.wait()

    prow = lax.broadcasted_iota(jnp.int32, (2 * NXC * NZL * CAP, 2 * NXC * NZL * CAP), 0)
    pcol = lax.broadcasted_iota(jnp.int32, (2 * NXC * NZL * CAP, 2 * NXC * NZL * CAP), 1)
    p_off = lax.div(prow, 2 * SLAB)
    p_kind = lax.rem(lax.div(prow, SLAB), 2)
    p_src = lax.rem(lax.div(prow, CAP), NXC)
    p_rank = lax.rem(prow, CAP)
    wanted = p_src * (2 * NZL * CAP) + p_kind * (NZL * CAP) + p_off * CAP + p_rank
    shuffle = jnp.where(pcol == wanted, 1.0, 0.0).astype(BF16)

    def shuffle_rows(c, carry):
        got = recv1[:, :, cols(c)].reshape(2 * NXC * NZL * CAP, CHUNK)
        moved = nn(shuffle, got).astype(BF16).reshape(NZL, 2, SLAB, CHUNK)
        perm[:, :, :, cols(c)] = moved
        rows[0, :, 0, :, cols(c)] = moved[0]
        return carry

    lax.fori_loop(0, chunks, shuffle_rows, 0)

    z_copies = [None]
    for k in range(1, NZ):
        copy = remote(
            perm.at[OFFSETS[k] % NZL], rows.at[k, :, 0], z_send.at[k], z_recv.at[k], at_z(OFFSETS[k])
        )
        copy.start()
        z_copies.append(copy)

    y_copies = {}
    f_copies = {}

    def forward(k):
        if k:
            z_copies[k].wait_recv()
        for way, (where, there) in enumerate(((up, 3), (dn, 1))):
            copy = remote(
                rows.at[k, :, 0], rows.at[k, :, there], y_send.at[way, k], y_recv.at[way, k], where
            )
            copy.start()
            y_copies[way, k] = copy

    def relay(k):
        way = k % 2
        y_copies[way, k].wait_recv()
        mine, where = ((3, up), (1, dn))[way]
        copy = remote(rows.at[k, :, mine], rows.at[k, :, 2], f_send.at[k], f_recv.at[k], where)
        copy.start()
        f_copies[k] = copy

    def arrived(g):
        for k in (2 * g, 2 * g + 1):
            y_copies[1 - k % 2, k].wait_recv()
            f_copies[k].wait_recv()

    group = 2 * NY * SLAB

    def compute(g):
        accs[...] = jnp.zeros_like(accs)

        def ahead(c, carry):
            tok = rows[2 * g : 2 * g + 2, 0, :, :, cols(c)].reshape(group, CHUNK)
            cts = rows[2 * g : 2 * g + 2, 1, :, :, cols(c)].reshape(group, CHUNK)
            accs[0] += nt(tok, pair[0, :, cols(c)])
            accs[1] += nt(tok, pair[1, :, cols(c)])
            accs[2] += nt(cts, down[:, cols(c)])
            return carry

        lax.fori_loop(0, chunks, ahead, 0)
        pre_gate, pre_up, hidden_grad = accs[0], accs[1], accs[2]
        sig = jax.nn.sigmoid(pre_gate)
        activated = pre_gate * sig
        hidden = (activated * pre_up).astype(BF16)
        gate_grad = (hidden_grad * pre_up * sig * (1.0 + pre_gate * (1.0 - sig))).astype(BF16)
        up_grad = (hidden_grad * activated).astype(BF16)
        span = slice(g * group, (g + 1) * group)
        gate_t[span, :] = gate_grad
        up_t[span, :] = up_grad
        hid_t[span, :] = hidden

        def behind(c, carry):
            got = nn(gate_grad, pair[0, :, cols(c)]) + nn(up_grad, pair[1, :, cols(c)])
            got = got.reshape(2, NY, SLAB, CHUNK)
            own[2 * g : 2 * g + 2, :, cols(c)] = got[:, 0]
            part[2 * g : 2 * g + 2, :, :, cols(c)] = got[:, 1:].astype(BF16)
            return carry

        lax.fori_loop(0, chunks, behind, 0)

    rl_copies = {}
    ru_copies = {}
    rd_copies = {}

    def give(k):
        if k % 2 == 0:
            rl = remote(part.at[k, 1], relayed.at[k], rl_send.at[k], rl_recv.at[k], up)
            direct = remote(part.at[k, 2], from_up.at[k], ru_send.at[k], ru_recv.at[k], dn)
            ru_copies[k] = direct
        else:
            rl = remote(part.at[k, 1], relayed.at[k], rl_send.at[k], rl_recv.at[k], dn)
            direct = remote(part.at[k, 0], from_down.at[k], rd_send.at[k], rd_recv.at[k], up)
            rd_copies[k] = direct
        rl.start()
        direct.start()
        rl_copies[k] = rl

    def give_on(k):
        rl_copies[k].wait_recv()
        mine = 0 if k % 2 == 0 else 2

        def add(c, carry):
            total = part[k, mine, :, cols(c)].astype(F32) + relayed[k, :, cols(c)].astype(F32)
            part[k, mine, :, cols(c)] = total.astype(BF16)
            return carry

        lax.fori_loop(0, chunks, add, 0)
        if k % 2 == 0:
            copy = remote(part.at[k, 0], from_down.at[k], rd_send.at[k], rd_recv.at[k], up)
            rd_copies[k] = copy
        else:
            copy = remote(part.at[k, 2], from_up.at[k], ru_send.at[k], ru_recv.at[k], dn)
            ru_copies[k] = copy
        copy.start()

    rz_copies = {}

    def settle(k):
        ru_copies[k].wait_recv()
        rd_copies[k].wait_recv()
        target = back if k == 0 else summed

        def add(c, carry):
            total = own[k, :, cols(c)] + (
                from_up[k, :, cols(c)].astype(F32) + from_down[k, :, cols(c)].astype(F32)
            )
            target[k, :, cols(c)] = total.astype(BF16)
            return carry

        lax.fori_loop(0, chunks, add, 0)
        if k:
            copy = remote(
                summed.at[k], back.at[k], rz_send.at[k], rz_recv.at[k], at_z(NZ - OFFSETS[k])
            )
            copy.start()
            rz_copies[k] = copy

    def weight_grads(which):
        def one(c, carry):
            kind = 0 if which < 2 else 1
            parts = [rows[2 * g : 2 * g + 2, kind, :, :, cols(c)].reshape(group, CHUNK) for g in range(4)]
            data = jnp.concatenate(parts, axis=0)
            got = tn((gate_t, up_t, hid_t)[which][...], data).astype(BF16)
            if which < 2:
                gpair[which, :, cols(c)] = got
            else:
                gdown[:, cols(c)] = got
            return carry

        lax.fori_loop(0, chunks, one, 0)
        if which < 2:
            copy = pltpu.make_async_copy(gpair.at[which], gpair_hbm.at[which], store_sem.at[which])
        else:
            copy = pltpu.make_async_copy(gdown, gdown_hbm, store_sem.at[which])
        copy.start()
        return copy

    forward(0)
    forward(1)
    forward(2)
    relay(0)
    relay(1)
    loads[2].wait()
    loads[3].wait()
    forward(3)
    relay(2)
    forward(4)
    relay(3)
    arrived(0)
    compute(0)
    give(0)
    give(1)
    forward(5)
    relay(4)
    forward(6)
    relay(5)
    arrived(1)
    compute(1)
    give(2)
    give(3)
    give_on(0)
    give_on(1)
    forward(7)
    relay(6)
    settle(0)
    settle(1)
    give_on(2)
    give_on(3)
    relay(7)
    arrived(2)
    compute(2)
    give(4)
    give(5)
    settle(2)
    settle(3)
    give_on(4)
    give_on(5)
    arrived(3)
    compute(3)
    give(6)
    give(7)
    settle(4)
    settle(5)
    stores = [weight_grads(0)]
    give_on(6)
    give_on(7)
    stores.append(weight_grads(1))
    settle(6)
    settle(7)
    stores.append(weight_grads(2))

    for k in range(1, NZ):
        rz_copies[k].wait_recv()
    half = NXC * NZL * CAP
    qrow = lax.broadcasted_iota(jnp.int32, (half, half), 0)
    qcol = lax.broadcasted_iota(jnp.int32, (half, half), 1)
    q_src = lax.div(qrow, NZL * CAP)
    q_off = lax.rem(lax.div(qrow, CAP), NZL)
    wanted_back = q_off * SLAB + q_src * CAP + lax.rem(qrow, CAP)
    shuffle_back = jnp.where(qcol == wanted_back, 1.0, 0.0).astype(BF16)

    def join(c, carry):
        parts = []
        for i in range(NZL):
            first, second = OFFSETS.index(i), OFFSETS.index(i + NZL)
            total = back[first, :, cols(c)].astype(F32) + back[second, :, cols(c)].astype(F32)
            parts.append(total.astype(BF16))
        moved = nn(shuffle_back, jnp.concatenate(parts, axis=0))
        for i in range(NXC):
            xsend[i, :, cols(c)] = moved[i * NZL * CAP : (i + 1) * NZL * CAP].astype(BF16)
        return carry

    lax.fori_loop(0, chunks, join, 0)

    rx_copies = []
    for i in range(1, NXC):
        copy = remote(
            xsend.at[i], final.at[xc], rx_send.at[i], rx_recv.at[i], at_x(NXC - i)
        )
        copy.start()
        rx_copies.append(copy)
    own_back = pltpu.make_async_copy(xsend.at[0], final.at[xc], load_sem.at[5])
    own_back.start()
    for copy in rx_copies:
        copy.wait_recv()
    own_back.wait()

    def place_out(c, carry):
        parts = [final[i, :, cols(c)].astype(F32) for i in range(NXC)]
        data = jnp.concatenate(parts, axis=0).astype(BF16)
        outv[:, cols(c)] = tn(pick_out, data).astype(BF16)
        return carry

    lax.fori_loop(0, chunks, place_out, 0)
    out_copy = pltpu.make_async_copy(outv, out_hbm, store_sem.at[3])
    out_copy.start()

    for copy in x_copies + z_copies[1:] + list(y_copies.values()) + list(f_copies.values()):
        copy.wait_send()
    for table in (rl_copies, ru_copies, rd_copies, rz_copies):
        for copy in table.values():
            copy.wait_send()
    for copy in rx_copies:
        copy.wait_send()
    for copy in stores:
        copy.wait()
    out_copy.wait()


def per_device(activations, cotangent, expert_ids, gate_probs, gate_up, down_proj):
    tokens, width = activations.shape
    units = down_proj.shape[1]
    pair = jnp.swapaxes(gate_up[0], 1, 2)
    down = down_proj[0]
    dma = pltpu.SemaphoreType.DMA
    vmem = pltpu.VMEM
    any_space = pl.BlockSpec(memory_space=pl.ANY)
    in_vmem = pl.BlockSpec(memory_space=pltpu.VMEM)
    total_rows = NZ * NY * SLAB
    out, gpair, gdown = pl.pallas_call(
        kernel,
        out_shape=(
            jax.ShapeDtypeStruct((tokens, width), BF16),
            jax.ShapeDtypeStruct((2, units, width), BF16),
            jax.ShapeDtypeStruct((units, width), BF16),
        ),
        in_specs=[in_vmem, in_vmem, any_space, any_space, any_space, any_space],
        out_specs=(any_space, any_space, any_space),
        scratch_shapes=[
            vmem((tokens, width), BF16),
            vmem((tokens, width), BF16),
            vmem((2, units, width), BF16),
            vmem((units, width), BF16),
            vmem((NXC, 2 * NZL * CAP, width), BF16),
            vmem((NXC, 2 * NZL * CAP, width), BF16),
            vmem((NZL, 2, SLAB, width), BF16),
            vmem((NZ, 2, NY, SLAB, width), BF16),
            vmem((3, 2 * NY * SLAB, units), F32),
            vmem((total_rows, units), BF16),
            vmem((total_rows, units), BF16),
            vmem((total_rows, units), BF16),
            vmem((NZ, SLAB, width), F32),
            vmem((NZ, NY - 1, SLAB, width), BF16),
            vmem((NZ, SLAB, width), BF16),
            vmem((NZ, SLAB, width), BF16),
            vmem((NZ, SLAB, width), BF16),
            vmem((NZ, SLAB, width), BF16),
            vmem((NZ, SLAB, width), BF16),
            vmem((NXC, NZL * CAP, width), BF16),
            vmem((NXC, NZL * CAP, width), BF16),
            vmem((tokens, width), BF16),
            vmem((2, units, width), BF16),
            vmem((units, width), BF16),
            dma((6,)),
            dma((4,)),
            dma((NXC,)),
            dma((NXC,)),
            dma((NZ,)),
            dma((NZ,)),
            dma((2, NZ)),
            dma((2, NZ)),
            dma((NZ,)),
            dma((NZ,)),
            dma((NZ,)),
            dma((NZ,)),
            dma((NZ,)),
            dma((NZ,)),
            dma((NZ,)),
            dma((NZ,)),
            dma((NZ,)),
            dma((NZ,)),
            dma((NXC,)),
            dma((NXC,)),
        ],
        compiler_params=pltpu.CompilerParams(
            collective_id=0, has_side_effects=True, vmem_limit_bytes=60 * 1024 * 1024
        ),
    )(expert_ids.reshape(1, tokens), gate_probs, activations, cotangent, pair, down)
    return out, jnp.swapaxes(gpair, 1, 2)[None], gdown[None]


def solution(mesh):
    in_specs = (
        P(("dp", "expert"), None),
        P(("dp", "expert"), None),
        P(("dp", "expert"), None),
        P(("dp", "expert"), None),
        P("expert", None, None, "dp"),
        P("expert", "dp", None),
    )
    out_specs = (P(("dp", "expert"), None), P("expert", None, None, "dp"), P("expert", "dp", None))
    return jax.shard_map(
        per_device, mesh=mesh, in_specs=in_specs, out_specs=out_specs, check_vma=False
    )
```

time: 566 us -> 172 us (0.30)
  waiting for transfers between devices: 391 us -> 0 us
  Pallas kernels: 0 us -> 162 us
  blocking collectives: 57.8 us -> 0 us
  local copies, waits for them, and re-layouts: 49.9 us -> 8.85 us
  other arithmetic: 22.6 us -> 0 us
  matrix products: 20.2 us -> 0 us
  between operations: 14.5 us -> 0.64 us
  starting transfers between devices: 8.24 us -> 0 us
    reduce_scatter x1 -> x0, waiting for transfers between devices: 216 us -> none  [per_device(): lax.psum_scatter(partial_value, 'dp', scatter_dimension=0, tiled=True)]
    all_gather x2 -> x0, waiting for transfers between devices: 165 us -> none  [the longest x1 96.6 us: per_device(): lax.all_gather(got_tok, 'dp', axis=0, tiled=True)]
    pallas_call x0 -> x1, Pallas kernels: none -> 162 us  [per_device(): pl.pallas_call(kernel, out_shape=(jax.ShapeDtypeStruct((tokens, width), B...]
    all_to_all x2 -> x0, blocking collectives: 57.8 us -> none  [the longest x1 31.5 us: per_device(): lax.all_to_all(send_tok, 'expert', split_axis=0, concat_axis=0, tiled=True)]
    dot_general x11 -> x0, matrix products: 20.2 us -> none  [the longest x7 14.4 us: contract(): lax.dot_general(left, right, (((left_dim,), (right_dim,)), ((), ())), pre...]
    gather x2 -> x0, local copies, waits for them, and re-layouts: 14.5 us -> none  [the longest x1 7.93 us: advance(): part_cot = jnp.take(rows_cot, picked, axis=0)]
    scatter x1 -> x0, local copies, waits for them, and re-layouts: 11.1 us -> none  [advance(): input_all = input_all.at[picked].set(input_rows)]
    all_to_all x1 -> x0, waiting for transfers between devices: 9.83 us -> none  [per_device(): lax.all_to_all(rounded, 'expert', split_axis=0, concat_axis=0, tiled=True)]
  transfers between devices with their start and end apart: 4 -> 0, of which waited for: 4 -> 0; matrix products, arithmetic and copies ran while one was open for 4% -> 0% of each run, Pallas kernels for 0% -> 0%
where the time goes in v1:
time: 172 us; the launch traced here: 171 us
  Pallas kernels  162 us (94%)
  local copies, waits for them, and re-layouts  8.85 us (5%)
    pallas_call x1, Pallas kernels, per_device(): pl.pallas_call(kernel, out_shape=(jax.ShapeDtypeStruct((tokens, width), B...  162 us
    unnamed x6, local copies, waits for them, and re-layouts  8.85 us

profile of v1, /device:TPU:1, one launch (start us, length us, event | category | flops | bytes accessed | tf_op | source)
XLA Modules:
  0.0 171.2 jit_solution(11884807167746435022)
XLA Ops:
  0.6 1.4 copy.9.probs_ref
  2.0 161.7 %shard_map.85 = (bf16[128,4096]{1,0:T(8,128)(2,1)}, bf16[2,192,4096]{2,1,0:T(8,128)(2,1)}, bf16[192,4096]{1,0:T(8,128)(2,1)}) custom-call(s32[1,128]{1,0:T(1,128)} %bitcast.13, f32[128,1]{1,0:T(8,128)} %copy.9.probs_ref, bf16[128,4096]{1,0:T(8,128)(2,1)} %act_hbm.1, bf16[128,4096]{1,0:T(8,128)(2,1)} %cot_hbm.1, bf16[2,192,4096]{2,1,0:T(8,128)(2,1)} %bitcast.9, ...), custom_call_target="tpu_custom_call" | custom-call | tf_op jit(solution)/shard_map/pallas_call | solution.py:463
  163.8 2.3 %copy.13 = bf16[128,4096]{1,0:T(8,128)(2,1)} copy(bf16[128,4096]{1,0:T(8,128)(2,1)} %get-tuple-element.12) | data formatting | bytes 2097152
  166.1 0.0 copy-start
  166.1 4.0 %copy.14 = bf16[1,2,4096,192]{2,3,1,0:T(8,128)(2,1)} copy(bf16[1,2,4096,192]{2,3,1,0:T(8,128)(2,1)} %bitcast.10) | data formatting | bytes 6291456
  170.1 0.0 copy-done
  170.1 1.1 copy.15
Async XLA Ops:
  166.1 4.0 %copy-start = (bf16[192,4096]{1,0:T(8,128)(2,1)S(1)}, bf16[192,4096]{1,0:T(8,128)(2,1)}, u32[]{:S(2)}) copy-start(bf16[192,4096]{1,0:T(8,128)(2,1)} %get-tuple-element.8) | copy-start | bytes 4718596

commit v2 on v1

v2 whole, which is shorter than its diff:
```python
import jax
import jax.numpy as jnp
from jax import lax
from jax.experimental import pallas as pl
from jax.experimental.pallas import tpu as pltpu
from jax.sharding import PartitionSpec as P

CAP = 2
MESH = pl.DeviceIdType.MESH
F32 = jnp.float32
BF16 = jnp.bfloat16

NY = 4
NZH = 2
NZL = 4
NZ = NZH * NZL
NXC = 8
SLAB = NXC * CAP
OFFSETS = (0, 1, 6, 2, 4, 5, 3, 7)
CHUNK = 512
HALVES = 2


def nt(left, right):
    return lax.dot_general(left, right, (((1,), (1,)), ((), ())), preferred_element_type=F32)


def nn(left, right):
    return lax.dot_general(left, right, (((1,), (0,)), ((), ())), preferred_element_type=F32)


def tn(left, right):
    return lax.dot_general(left, right, (((0,), (0,)), ((), ())), preferred_element_type=F32)


def kernel(
    ids_ref,
    probs_ref,
    act_hbm,
    cot_hbm,
    pair_hbm,
    down_hbm,
    pick_ref,
    final,
    gpair_hbm,
    gdown_hbm,
    act,
    cot,
    pair,
    down,
    send,
    recv1,
    perm,
    rows,
    accs,
    gate_t,
    up_t,
    hid_t,
    own,
    part,
    relayed,
    from_up,
    from_down,
    summed,
    back,
    xsend,
    gpair,
    gdown,
    load_sem,
    store_sem,
    x_send,
    x_recv,
    z_send,
    z_recv,
    y_send,
    y_recv,
    f_send,
    f_recv,
    rl_send,
    rl_recv,
    ru_send,
    ru_recv,
    rd_send,
    rd_recv,
    rz_send,
    rz_recv,
    rx_send,
    rx_recv,
):
    width = act.shape[1]
    chunks = width // CHUNK
    half_width = width // HALVES
    half_chunks = chunks // HALVES
    halves = range(HALVES)
    tokens = act.shape[0]
    e = lax.axis_index("expert")
    d = lax.axis_index("dp")
    zl = lax.div(e, NXC)
    xc = lax.rem(e, NXC)
    y = lax.div(d, NZH)
    z = lax.rem(d, NZH) * NZL + zl

    def dev(yy, zz, xx):
        return (yy * NZH + lax.div(zz, NZL), lax.rem(zz, NZL) * NXC + xx)

    def at_x(i):
        return dev(y, z, lax.rem(xc + i, NXC))

    def at_z(i):
        return dev(y, lax.rem(z + i, NZ), xc)

    up = dev(lax.rem(y + 1, NY), z, xc)
    dn = dev(lax.rem(y + NY - 1, NY), z, xc)

    def cols(c):
        return pl.ds(pl.multiple_of(c * CHUNK, CHUNK), CHUNK)

    def piece(h):
        return pl.ds(h * half_width, half_width)

    def over(h, body):
        lax.fori_loop(h * half_chunks, (h + 1) * half_chunks, body, 0)

    def remote(src, dst, ssem, rsem, where):
        return pltpu.make_async_remote_copy(
            src_ref=src, dst_ref=dst, send_sem=ssem, recv_sem=rsem, device_id=where, device_id_type=MESH
        )

    loads = [
        pltpu.make_async_copy(act_hbm, act, load_sem.at[0]),
        pltpu.make_async_copy(cot_hbm, cot, load_sem.at[1]),
        pltpu.make_async_copy(pair_hbm, pair, load_sem.at[2]),
        pltpu.make_async_copy(down_hbm, down, load_sem.at[3]),
    ]
    for copy in loads:
        copy.start()
    barrier = pltpu.get_barrier_semaphore()
    partners = [at_x(i) for i in range(1, NXC)] + [at_z(i) for i in range(1, NZ)] + [up, dn]
    for partner in partners:
        pl.semaphore_signal(barrier, inc=1, device_id=partner, device_id_type=MESH)

    ids = ids_ref[...]
    ids_wide = jnp.broadcast_to(ids.astype(F32), (tokens, tokens))
    ids_tall = ids_wide.T
    row_at = lax.broadcasted_iota(jnp.int32, (tokens, tokens), 0)
    col_at = lax.broadcasted_iota(jnp.int32, (tokens, tokens), 1)
    earlier = jnp.where((ids_wide == ids_tall) & (row_at < col_at), 1.0, 0.0)
    rank = jnp.sum(earlier, axis=0, keepdims=True).astype(jnp.int32)
    offset = lax.rem(lax.div(ids, NXC) + NZL - zl, NZL)
    inside = ids < NZL * NXC
    place = lax.rem(ids, NXC) * (2 * NZL * CAP) + offset * CAP + rank
    place = jnp.where(inside, place, -1024)
    pick_tok = jnp.where(row_at == place, 1.0, 0.0).astype(BF16)
    pick_cot = jnp.where(row_at == place + NZL * CAP, 1.0, 0.0).astype(BF16)
    slot = lax.rem(ids, NXC) * (NZL * CAP) + offset * CAP + rank
    slot = jnp.where(inside, slot, -1024)
    half_row = lax.broadcasted_iota(jnp.int32, (NXC * NZL * CAP, tokens), 0)
    pick_ref[...] = jnp.where(half_row == slot, 1.0, 0.0).astype(BF16)

    loads[0].wait()
    loads[1].wait()
    probs = jnp.broadcast_to(probs_ref[...], (tokens, tokens)).T[:, :1]

    def gather_rows(c, carry):
        scaled = (probs * cot[:, cols(c)].astype(F32)).astype(BF16)
        got = nn(pick_tok, act[:, cols(c)]) + nn(pick_cot, scaled)
        got = got.astype(BF16).reshape(NXC, 2 * NZL * CAP, CHUNK)
        send[:, :, cols(c)] = got
        return carry

    lax.fori_loop(0, chunks, gather_rows, 0)
    pl.semaphore_wait(barrier, len(partners))

    x_copies = {}
    for h in halves:
        for i in range(1, NXC):
            copy = remote(
                send.at[lax.rem(xc + i, NXC), :, piece(h)],
                recv1.at[i, :, piece(h)],
                x_send.at[h, i],
                x_recv.at[h, i],
                at_x(i),
            )
            copy.start()
            x_copies[h, i] = copy
    own_copy = pltpu.make_async_copy(send.at[xc], recv1.at[0], load_sem.at[4])
    own_copy.start()

    prow = lax.broadcasted_iota(jnp.int32, (2 * NXC * NZL * CAP, 2 * NXC * NZL * CAP), 0)
    pcol = lax.broadcasted_iota(jnp.int32, (2 * NXC * NZL * CAP, 2 * NXC * NZL * CAP), 1)
    p_off = lax.div(prow, 2 * SLAB)
    p_kind = lax.rem(lax.div(prow, SLAB), 2)
    p_src = lax.rem(lax.div(prow, CAP), NXC)
    p_rank = lax.rem(prow, CAP)
    wanted = p_src * (2 * NZL * CAP) + p_kind * (NZL * CAP) + p_off * CAP + p_rank
    shuffle = jnp.where(pcol == wanted, 1.0, 0.0).astype(BF16)

    def shuffle_rows(c, carry):
        got = recv1[:, :, cols(c)].reshape(2 * NXC * NZL * CAP, CHUNK)
        moved = nn(shuffle, got).astype(BF16).reshape(NZL, 2, SLAB, CHUNK)
        perm[:, :, :, cols(c)] = moved
        rows[0, :, 0, :, cols(c)] = moved[0]
        return carry

    def cross(h):
        for i in range(1, NXC):
            x_copies[h, i].wait_recv()
        over(h, shuffle_rows)

    z_copies = {}

    def spread(k, h):
        copy = remote(
            perm.at[OFFSETS[k] % NZL, :, :, piece(h)],
            rows.at[k, :, 0, :, piece(h)],
            z_send.at[h, k],
            z_recv.at[h, k],
            at_z(OFFSETS[k]),
        )
        copy.start()
        z_copies[k, h] = copy

    y_copies = {}
    f_copies = {}

    def forward(k, h):
        if k:
            z_copies[k, h].wait_recv()
        for way, (where, there) in enumerate(((up, 3), (dn, 1))):
            copy = remote(
                rows.at[k, :, 0, :, piece(h)],
                rows.at[k, :, there, :, piece(h)],
                y_send.at[way, h, k],
                y_recv.at[way, h, k],
                where,
            )
            copy.start()
            y_copies[way, k, h] = copy

    def relay(k, h):
        way = k % 2
        y_copies[way, k, h].wait_recv()
        mine, where = ((3, up), (1, dn))[way]
        copy = remote(
            rows.at[k, :, mine, :, piece(h)],
            rows.at[k, :, 2, :, piece(h)],
            f_send.at[h, k],
            f_recv.at[h, k],
            where,
        )
        copy.start()
        f_copies[k, h] = copy

    def arrived(k):
        for h in halves:
            y_copies[1 - k % 2, k, h].wait_recv()
            f_copies[k, h].wait_recv()

    per_slab = NY * SLAB

    def compute(k, count):
        group = count * per_slab
        accs[:, :group] = jnp.zeros((3, group, accs.shape[2]), F32)

        def ahead(c, carry):
            tok = rows[k : k + count, 0, :, :, cols(c)].reshape(group, CHUNK)
            cts = rows[k : k + count, 1, :, :, cols(c)].reshape(group, CHUNK)
            accs[0, :group] += nt(tok, pair[0, :, cols(c)])
            accs[1, :group] += nt(tok, pair[1, :, cols(c)])
            accs[2, :group] += nt(cts, down[:, cols(c)])
            return carry

        lax.fori_loop(0, chunks, ahead, 0)
        pre_gate, pre_up, hidden_grad = accs[0, :group], accs[1, :group], accs[2, :group]
        sig = jax.nn.sigmoid(pre_gate)
        activated = pre_gate * sig
        hidden = (activated * pre_up).astype(BF16)
        gate_grad = (hidden_grad * pre_up * sig * (1.0 + pre_gate * (1.0 - sig))).astype(BF16)
        up_grad = (hidden_grad * activated).astype(BF16)
        span = slice(k * per_slab, (k + count) * per_slab)
        gate_t[span, :] = gate_grad
        up_t[span, :] = up_grad
        hid_t[span, :] = hidden

        def behind(c, carry):
            got = nn(gate_grad, pair[0, :, cols(c)]) + nn(up_grad, pair[1, :, cols(c)])
            got = got.reshape(count, NY, SLAB, CHUNK)
            own[k : k + count, :, cols(c)] = got[:, 0]
            part[k : k + count, :, :, cols(c)] = got[:, 1:].astype(BF16)
            return carry

        for h in halves:
            over(h, behind)
            for i in range(count):
                give(k + i, h)

    rl_copies = {}
    ru_copies = {}
    rd_copies = {}

    def to_upper(k, h):
        copy = remote(
            part.at[k, 0, :, piece(h)],
            from_down.at[k, :, piece(h)],
            rd_send.at[h, k],
            rd_recv.at[h, k],
            up,
        )
        copy.start()
        rd_copies[k, h] = copy

    def to_lower(k, h):
        copy = remote(
            part.at[k, 2, :, piece(h)],
            from_up.at[k, :, piece(h)],
            ru_send.at[h, k],
            ru_recv.at[h, k],
            dn,
        )
        copy.start()
        ru_copies[k, h] = copy

    def give(k, h):
        copy = remote(
            part.at[k, 1, :, piece(h)],
            relayed.at[k, :, piece(h)],
            rl_send.at[h, k],
            rl_recv.at[h, k],
            (up, dn)[k % 2],
        )
        copy.start()
        rl_copies[k, h] = copy
        (to_lower, to_upper)[k % 2](k, h)

    def give_on(k, h):
        rl_copies[k, h].wait_recv()
        mine = (0, 2)[k % 2]

        def add(c, carry):
            total = part[k, mine, :, cols(c)].astype(F32) + relayed[k, :, cols(c)].astype(F32)
            part[k, mine, :, cols(c)] = total.astype(BF16)
            return carry

        over(h, add)
        (to_upper, to_lower)[k % 2](k, h)

    rz_copies = {}

    def settle(k, h):
        ru_copies[k, h].wait_recv()
        rd_copies[k, h].wait_recv()
        target = back if k == 0 else summed

        def add(c, carry):
            total = own[k, :, cols(c)] + (
                from_up[k, :, cols(c)].astype(F32) + from_down[k, :, cols(c)].astype(F32)
            )
            target[k, :, cols(c)] = total.astype(BF16)
            return carry

        over(h, add)
        if k:
            copy = remote(
                summed.at[k, :, piece(h)],
                back.at[k, :, piece(h)],
                rz_send.at[h, k],
                rz_recv.at[h, k],
                at_z(NZ - OFFSETS[k]),
            )
            copy.start()
            rz_copies[k, h] = copy

    def weight_grads(which):
        def one(c, carry):
            kind = 0 if which < 2 else 1
            data = rows[:, kind, :, :, cols(c)].reshape(NZ * per_slab, CHUNK)
            got = tn((gate_t, up_t, hid_t)[which][...], data).astype(BF16)
            if which < 2:
                gpair[which, :, cols(c)] = got
            else:
                gdown[:, cols(c)] = got
            return carry

        lax.fori_loop(0, chunks, one, 0)
        if which < 2:
            copy = pltpu.make_async_copy(gpair.at[which], gpair_hbm.at[which], store_sem.at[which])
        else:
            copy = pltpu.make_async_copy(gdown, gdown_hbm, store_sem.at[which])
        copy.start()
        return copy

    own_copy.wait()
    cross(0)
    for k in (1, 2, 3):
        spread(k, 0)
    forward(0, 0)
    relay(0, 0)
    forward(1, 0)
    cross(1)
    for k in (1, 2, 3):
        spread(k, 1)
    forward(0, 1)
    for k in (4, 5, 6, 7):
        spread(k, 0)
        spread(k, 1)
    forward(2, 0)
    relay(1, 0)
    forward(1, 1)
    relay(0, 1)
    forward(3, 0)
    relay(2, 0)
    forward(2, 1)
    relay(1, 1)
    forward(3, 1)
    relay(3, 0)
    relay(2, 1)
    loads[2].wait()
    loads[3].wait()

    def both(do, *slabs):
        for k in slabs:
            for h in halves:
                do(k, h)

    both(forward, 4)
    arrived(0)
    arrived(1)
    compute(0, 2)
    relay(3, 1)
    both(relay, 4)
    both(forward, 5)
    both(give_on, 0, 1)
    both(relay, 5)
    both(forward, 6)
    arrived(2)
    arrived(3)
    compute(2, 2)
    both(settle, 0, 1)
    both(relay, 6)
    both(forward, 7)
    both(give_on, 2, 3)
    arrived(4)
    arrived(5)
    compute(4, 2)
    both(settle, 2, 3)
    both(relay, 7)
    both(give_on, 4, 5)
    arrived(6)
    compute(6, 1)
    both(settle, 4, 5)
    arrived(7)
    compute(7, 1)
    both(give_on, 6)
    both(settle, 6)
    stores = [weight_grads(0)]
    both(give_on, 7)
    stores.append(weight_grads(1))
    both(settle, 7)
    stores.append(weight_grads(2))

    half = NXC * NZL * CAP
    qrow = lax.broadcasted_iota(jnp.int32, (half, half), 0)
    qcol = lax.broadcasted_iota(jnp.int32, (half, half), 1)
    q_src = lax.div(qrow, NZL * CAP)
    q_off = lax.rem(lax.div(qrow, CAP), NZL)
    wanted_back = q_off * SLAB + q_src * CAP + lax.rem(qrow, CAP)
    shuffle_back = jnp.where(qcol == wanted_back, 1.0, 0.0).astype(BF16)

    def join(c, carry):
        parts = []
        for i in range(NZL):
            first, second = OFFSETS.index(i), OFFSETS.index(i + NZL)
            total = back[first, :, cols(c)].astype(F32) + back[second, :, cols(c)].astype(F32)
            parts.append(total.astype(BF16))
        moved = nn(shuffle_back, jnp.concatenate(parts, axis=0))
        for i in range(NXC):
            xsend[i, :, cols(c)] = moved[i * NZL * CAP : (i + 1) * NZL * CAP].astype(BF16)
        return carry

    rx_copies = []
    own_back = []
    for h in halves:
        for k in range(1, NZ):
            rz_copies[k, h].wait_recv()
        over(h, join)
        for i in range(1, NXC):
            copy = remote(
                xsend.at[i, :, piece(h)],
                final.at[xc, :, piece(h)],
                rx_send.at[h, i],
                rx_recv.at[h, i],
                at_x(NXC - i),
            )
            copy.start()
            rx_copies.append(copy)
        copy = pltpu.make_async_copy(
            xsend.at[0, :, piece(h)], final.at[xc, :, piece(h)], store_sem.at[3 + h]
        )
        copy.start()
        own_back.append(copy)

    for table in (x_copies, z_copies, y_copies, f_copies, rl_copies, ru_copies, rd_copies, rz_copies):
        for copy in table.values():
            copy.wait_send()
    for copy in rx_copies:
        copy.wait()
    for copy in stores + own_back:
        copy.wait()


def per_device(activations, cotangent, expert_ids, gate_probs, gate_up, down_proj):
    tokens, width = activations.shape
    units = down_proj.shape[1]
    pair = jnp.swapaxes(gate_up[0], 1, 2)
    down = down_proj[0]
    dma = pltpu.SemaphoreType.DMA
    vmem = pltpu.VMEM
    any_space = pl.BlockSpec(memory_space=pl.ANY)
    in_vmem = pl.BlockSpec(memory_space=pltpu.VMEM)
    total_rows = NZ * NY * SLAB
    pick, final, gpair, gdown = pl.pallas_call(
        kernel,
        out_shape=(
            jax.ShapeDtypeStruct((NXC * NZL * CAP, tokens), BF16),
            jax.ShapeDtypeStruct((NXC, NZL * CAP, width), BF16),
            jax.ShapeDtypeStruct((2, units, width), BF16),
            jax.ShapeDtypeStruct((units, width), BF16),
        ),
        in_specs=[in_vmem, in_vmem, any_space, any_space, any_space, any_space],
        out_specs=(in_vmem, any_space, any_space, any_space),
        scratch_shapes=[
            vmem((tokens, width), BF16),
            vmem((tokens, width), BF16),
            vmem((2, units, width), BF16),
            vmem((units, width), BF16),
            vmem((NXC, 2 * NZL * CAP, width), BF16),
            vmem((NXC, 2 * NZL * CAP, width), BF16),
            vmem((NZL, 2, SLAB, width), BF16),
            vmem((NZ, 2, NY, SLAB, width), BF16),
            vmem((3, 2 * NY * SLAB, units), F32),
            vmem((total_rows, units), BF16),
            vmem((total_rows, units), BF16),
            vmem((total_rows, units), BF16),
            vmem((NZ, SLAB, width), F32),
            vmem((NZ, NY - 1, SLAB, width), BF16),
            vmem((NZ, SLAB, width), BF16),
            vmem((NZ, SLAB, width), BF16),
            vmem((NZ, SLAB, width), BF16),
            vmem((NZ, SLAB, width), BF16),
            vmem((NZ, SLAB, width), BF16),
            vmem((NXC, NZL * CAP, width), BF16),
            vmem((2, units, width), BF16),
            vmem((units, width), BF16),
            dma((5,)),
            dma((5,)),
            dma((HALVES, NXC)),
            dma((HALVES, NXC)),
            dma((HALVES, NZ)),
            dma((HALVES, NZ)),
            dma((2, HALVES, NZ)),
            dma((2, HALVES, NZ)),
            dma((HALVES, NZ)),
            dma((HALVES, NZ)),
            dma((HALVES, NZ)),
            dma((HALVES, NZ)),
            dma((HALVES, NZ)),
            dma((HALVES, NZ)),
            dma((HALVES, NZ)),
            dma((HALVES, NZ)),
            dma((HALVES, NZ)),
            dma((HALVES, NZ)),
            dma((HALVES, NXC)),
            dma((HALVES, NXC)),
        ],
        compiler_params=pltpu.CompilerParams(
            collective_id=0, has_side_effects=True, vmem_limit_bytes=60 * 1024 * 1024
        ),
    )(expert_ids.reshape(1, tokens), gate_probs.reshape(1, tokens), activations, cotangent, pair, down)
    out = tn(pick, final.reshape(NXC * NZL * CAP, width)).astype(BF16)
    return out, jnp.swapaxes(gpair, 1, 2)[None], gdown[None]


def solution(mesh):
    in_specs = (
        P(("dp", "expert"), None),
        P(("dp", "expert"), None),
        P(("dp", "expert"), None),
        P(("dp", "expert"), None),
        P("expert", None, None, "dp"),
        P("expert", "dp", None),
    )
    out_specs = (P(("dp", "expert"), None), P("expert", None, None, "dp"), P("expert", "dp", None))
    return jax.shard_map(
        per_device, mesh=mesh, in_specs=in_specs, out_specs=out_specs, check_vma=False
    )
```

time: 172 us -> 158 us (0.919)
  Pallas kernels: 162 us -> 150 us
  local copies, waits for them, and re-layouts: 8.85 us -> 5.17 us
  matrix products: 0 us -> 2.48 us
    pallas_call x1, Pallas kernels: 162 us -> 150 us  [per_device(): pl.pallas_call(kernel, out_shape=(jax.ShapeDtypeStruct((NXC * NZL * CAP,...]
    unnamed x6 -> x4, local copies, waits for them, and re-layouts: 8.85 us -> 5.17 us
    dot_general x0 -> x1, matrix products: none -> 2.48 us  [tn(): lax.dot_general(left, right, (((0,), (0,)), ((), ())), preferred_element_...]
where the time goes in v2:
time: 158 us
  Pallas kernels  150 us (95%)
  local copies, waits for them, and re-layouts  5.17 us (3%)
  matrix products  2.48 us (2%)
    pallas_call x1, Pallas kernels, per_device(): pl.pallas_call(kernel, out_shape=(jax.ShapeDtypeStruct((NXC * NZL * CAP,...  150 us
    unnamed x4, local copies, waits for them, and re-layouts  5.17 us

profile of v2, /device:TPU:1, one launch (start us, length us, event | category | flops | bytes accessed | tf_op | source)
XLA Modules:
  0.0 158.2 jit_solution(10161372774335962002)
XLA Ops:
  0.6 149.9 %shard_map.85 = (bf16[64,128]{1,0:T(8,128)(2,1)}, bf16[8,8,4096]{2,1,0:T(8,128)(2,1)}, bf16[2,192,4096]{2,1,0:T(8,128)(2,1)}, bf16[192,4096]{1,0:T(8,128)(2,1)}) custom-call(s32[1,128]{1,0:T(1,128)} %bitcast.18, f32[1,128]{1,0:T(1,128)} %bitcast.19, bf16[128,4096]{1,0:T(8,128)(2,1)} %act_hbm.1, bf16[128,4096]{1,0:T(8,128)(2,1)} %cot_hbm.1, ...), custom_call_target="tpu_custom_call" | custom-call | tf_op jit(solution)/shard_map/pallas_call | solution.py:521
  150.6 2.5 %convolution_convert_fusion = bf16[128,4096]{1,0:T(8,128)(2,1)} fusion(bf16[64,128]{1,0:T(8,128)(2,1)} %get-tuple-element.7, bf16[8,8,4096]{2,1,0:T(8,128)(2,1)} %get-tuple-element.8), kind=kOutput, calls=%fused_computation | convolution fusion | flops 67633152 | bytes 1589248 | tf_op jit(solution)/shard_map/dot_general | solution.py:33
  153.1 0.0 copy-start
  153.1 4.0 %copy.11 = bf16[1,2,4096,192]{2,3,1,0:T(8,128)(2,1)} copy(bf16[1,2,4096,192]{2,3,1,0:T(8,128)(2,1)} %bitcast.15) | data formatting | bytes 6291456
  157.1 0.0 copy-done
  157.1 1.1 copy.12
Async XLA Ops:
  153.1 4.0 %copy-start = (bf16[192,4096]{1,0:T(8,128)(2,1)S(1)}, bf16[192,4096]{1,0:T(8,128)(2,1)}, u32[]{:S(2)}) copy-start(bf16[192,4096]{1,0:T(8,128)(2,1)} %get-tuple-element.10) | copy-start | bytes 4718596

commit v3 on v2

--- a/solution.py
+++ b/solution.py
@@ -16,9 +16,110 @@
 NZ = NZH * NZL
 NXC = 8
 SLAB = NXC * CAP
-OFFSETS = (0, 1, 6, 2, 4, 5, 3, 7)
+OFFSETS = (0, 1, 7, 2, 6, 3, 5, 4)
 CHUNK = 512
-HALVES = 2
+X_PIECES = 4
+OUT_PIECES = (4, 2, 2, 2, 2, 2, 2, 2)
+BACK_PIECES = (2, 2, 2, 2, 2, 2, 2, 2)
+END_PIECES = 2
+MOST = 4
+ORDER = (
+    ('cross', 0),
+    ('forward', 0, 0),
+    ('cross', 1),
+    ('spread', 3, 0),
+    ('forward', 0, 1),
+    ('spread', 2, 0),
+    ('cross', 2),
+    ('spread', 1, 0),
+    ('spread', 6, 0),
+    ('spread', 4, 0),
+    ('spread', 5, 0),
+    ('forward', 0, 2),
+    ('relay', 0, 1),
+    ('cross', 3),
+    ('forward', 0, 3),
+    ('spread', 2, 1),
+    ('forward', 2, 0),
+    ('spread', 5, 1),
+    ('relay', 0, 0),
+    ('forward', 3, 0),
+    ('spread', 1, 1),
+    ('forward', 1, 0),
+    ('relay', 3, 0),
+    ('relay', 0, 2),
+    ('relay', 2, 0),
+    ('spread', 4, 1),
+    ('spread', 7, 0),
+    ('spread', 6, 1),
+    ('relay', 1, 0),
+    ('forward', 4, 0),
+    ('forward', 2, 1),
+    ('relay', 0, 3),
+    ('forward', 6, 0),
+    ('forward', 5, 0),
+    ('forward', 4, 1),
+    ('relay', 2, 1),
+    ('forward', 5, 1),
+    ('relay', 4, 0),
+    ('relay', 5, 0),
+    ('spread', 7, 1),
+    ('forward', 1, 1),
+    ('relay', 5, 1),
+    ('relay', 4, 1),
+    ('forward', 7, 0),
+    ('spread', 3, 1),
+    ('relay', 1, 1),
+    ('forward', 6, 1),
+    ('relay', 6, 0),
+    ('forward', 7, 1),
+    ('relay', 7, 0),
+    ('relay', 7, 1),
+    ('relay', 6, 1),
+    ('forward', 3, 1),
+    ('compute', 4, 2),
+    ('compute', 6, 2),
+    ('give_on', 4, 0),
+    ('give_on', 5, 0),
+    ('give_on', 7, 0),
+    ('relay', 3, 1),
+    ('give_on', 5, 1),
+    ('give_on', 6, 0),
+    ('compute', 0, 2),
+    ('give_on', 6, 1),
+    ('settle', 5, 0),
+    ('settle', 4, 0),
+    ('give_on', 4, 1),
+    ('give_on', 7, 1),
+    ('settle', 7, 0),
+    ('settle', 6, 0),
+    ('compute', 2, 2),
+    ('grads', 2),
+    ('settle', 4, 1),
+    ('give_on', 0, 1),
+    ('settle', 5, 1),
+    ('give_on', 3, 0),
+    ('settle', 7, 1),
+    ('settle', 6, 1),
+    ('give_on', 0, 0),
+    ('give_on', 1, 0),
+    ('give_on', 2, 0),
+    ('give_on', 2, 1),
+    ('give_on', 3, 1),
+    ('give_on', 1, 1),
+    ('settle', 3, 0),
+    ('settle', 1, 0),
+    ('settle', 0, 1),
+    ('settle', 2, 0),
+    ('settle', 0, 0),
+    ('settle', 3, 1),
+    ('settle', 1, 1),
+    ('settle', 2, 1),
+    ('join', 0),
+    ('grads', 0),
+    ('join', 1),
+    ('grads', 1),
+)
 
 
 def nt(left, right):
@@ -42,8 +143,8 @@
     down_hbm,
     pick_ref,
     final,
-    gpair_hbm,
-    gdown_hbm,
+    gpair,
+    gdown,
     act,
     cot,
     pair,
@@ -64,8 +165,6 @@
     summed,
     back,
     xsend,
-    gpair,
-    gdown,
     load_sem,
     store_sem,
     x_send,
@@ -89,9 +188,6 @@
 ):
     width = act.shape[1]
     chunks = width // CHUNK
-    half_width = width // HALVES
-    half_chunks = chunks // HALVES
-    halves = range(HALVES)
     tokens = act.shape[0]
     e = lax.axis_index("expert")
     d = lax.axis_index("dp")
@@ -115,11 +211,11 @@
     def cols(c):
         return pl.ds(pl.multiple_of(c * CHUNK, CHUNK), CHUNK)
 
-    def piece(h):
-        return pl.ds(h * half_width, half_width)
-
-    def over(h, body):
-        lax.fori_loop(h * half_chunks, (h + 1) * half_chunks, body, 0)
+    def piece(count, h):
+        return pl.ds(h * (width // count), width // count)
+
+    def over(count, h, body):
+        lax.fori_loop(h * chunks // count, (h + 1) * chunks // count, body, 0)
 
     def remote(src, dst, ssem, rsem, where):
         return pltpu.make_async_remote_copy(
@@ -135,7 +231,8 @@
     for copy in loads:
         copy.start()
     barrier = pltpu.get_barrier_semaphore()
-    partners = [at_x(i) for i in range(1, NXC)] + [at_z(i) for i in range(1, NZ)] + [up, dn]
+    far_first = (4, 3, 5, 2, 6, 1, 7)
+    partners = [at_z(i) for i in far_first] + [at_x(i) for i in (4, 5, 2, 3, 6, 7, 1)] + [up, dn]
     for partner in partners:
         pl.semaphore_signal(barrier, inc=1, device_id=partner, device_id_type=MESH)
 
@@ -172,11 +269,11 @@
     pl.semaphore_wait(barrier, len(partners))
 
     x_copies = {}
-    for h in halves:
+    for h in range(X_PIECES):
         for i in range(1, NXC):
             copy = remote(
-                send.at[lax.rem(xc + i, NXC), :, piece(h)],
-                recv1.at[i, :, piece(h)],
+                send.at[lax.rem(xc + i, NXC), :, piece(X_PIECES, h)],
+                recv1.at[i, :, piece(X_PIECES, h)],
                 x_send.at[h, i],
                 x_recv.at[h, i],
                 at_x(i),
@@ -203,16 +300,18 @@
         return carry
 
     def cross(h):
+        if h == 0:
+            own_copy.wait()
         for i in range(1, NXC):
             x_copies[h, i].wait_recv()
-        over(h, shuffle_rows)
+        over(X_PIECES, h, shuffle_rows)
 
     z_copies = {}
 
     def spread(k, h):
         copy = remote(
-            perm.at[OFFSETS[k] % NZL, :, :, piece(h)],
-            rows.at[k, :, 0, :, piece(h)],
+            perm.at[OFFSETS[k] % NZL, :, :, piece(OUT_PIECES[k], h)],
+            rows.at[k, :, 0, :, piece(OUT_PIECES[k], h)],
             z_send.at[h, k],
             z_recv.at[h, k],
             at_z(OFFSETS[k]),
@@ -228,8 +327,8 @@
             z_copies[k, h].wait_recv()
         for way, (where, there) in enumerate(((up, 3), (dn, 1))):
             copy = remote(
-                rows.at[k, :, 0, :, piece(h)],
-                rows.at[k, :, there, :, piece(h)],
+                rows.at[k, :, 0, :, piece(OUT_PIECES[k], h)],
+                rows.at[k, :, there, :, piece(OUT_PIECES[k], h)],
                 y_send.at[way, h, k],
                 y_recv.at[way, h, k],
                 where,
@@ -242,8 +341,8 @@
         y_copies[way, k, h].wait_recv()
         mine, where = ((3, up), (1, dn))[way]
         copy = remote(
-            rows.at[k, :, mine, :, piece(h)],
-            rows.at[k, :, 2, :, piece(h)],
+            rows.at[k, :, mine, :, piece(OUT_PIECES[k], h)],
+            rows.at[k, :, 2, :, piece(OUT_PIECES[k], h)],
             f_send.at[h, k],
             f_recv.at[h, k],
             where,
@@ -252,13 +351,15 @@
         f_copies[k, h] = copy
 
     def arrived(k):
-        for h in halves:
+        for h in range(OUT_PIECES[k]):
             y_copies[1 - k % 2, k, h].wait_recv()
             f_copies[k, h].wait_recv()
 
     per_slab = NY * SLAB
 
     def compute(k, count):
+        for i in range(count):
+            arrived(k + i)
         group = count * per_slab
         accs[:, :group] = jnp.zeros((3, group, accs.shape[2]), F32)
 
@@ -289,8 +390,8 @@
             part[k : k + count, :, :, cols(c)] = got[:, 1:].astype(BF16)
             return carry
 
-        for h in halves:
-            over(h, behind)
+        for h in range(BACK_PIECES[k]):
+            over(BACK_PIECES[k], h, behind)
             for i in range(count):
                 give(k + i, h)
 
@@ -300,8 +401,8 @@
 
     def to_upper(k, h):
         copy = remote(
-            part.at[k, 0, :, piece(h)],
-            from_down.at[k, :, piece(h)],
+            part.at[k, 0, :, piece(BACK_PIECES[k], h)],
+            from_down.at[k, :, piece(BACK_PIECES[k], h)],
             rd_send.at[h, k],
             rd_recv.at[h, k],
             up,
@@ -311,8 +412,8 @@
 
     def to_lower(k, h):
         copy = remote(
-            part.at[k, 2, :, piece(h)],
-            from_up.at[k, :, piece(h)],
+            part.at[k, 2, :, piece(BACK_PIECES[k], h)],
+            from_up.at[k, :, piece(BACK_PIECES[k], h)],
             ru_send.at[h, k],
             ru_recv.at[h, k],
             dn,
@@ -322,8 +423,8 @@
 
     def give(k, h):
         copy = remote(
-            part.at[k, 1, :, piece(h)],
-            relayed.at[k, :, piece(h)],
+            part.at[k, 1, :, piece(BACK_PIECES[k], h)],
+            relayed.at[k, :, piece(BACK_PIECES[k], h)],
             rl_send.at[h, k],
             rl_recv.at[h, k],
             (up, dn)[k % 2],
@@ -341,7 +442,7 @@
             part[k, mine, :, cols(c)] = total.astype(BF16)
             return carry
 
-        over(h, add)
+        over(BACK_PIECES[k], h, add)
         (to_upper, to_lower)[k % 2](k, h)
 
     rz_copies = {}
@@ -358,11 +459,11 @@
             target[k, :, cols(c)] = total.astype(BF16)
             return carry
 
-        over(h, add)
+        over(BACK_PIECES[k], h, add)
         if k:
             copy = remote(
-                summed.at[k, :, piece(h)],
-                back.at[k, :, piece(h)],
+                summed.at[k, :, piece(BACK_PIECES[k], h)],
+                back.at[k, :, piece(BACK_PIECES[k], h)],
                 rz_send.at[h, k],
                 rz_recv.at[h, k],
                 at_z(NZ - OFFSETS[k]),
@@ -370,7 +471,7 @@
             copy.start()
             rz_copies[k, h] = copy
 
-    def weight_grads(which):
+    def grads(which):
         def one(c, carry):
             kind = 0 if which < 2 else 1
             data = rows[:, kind, :, :, cols(c)].reshape(NZ * per_slab, CHUNK)
@@ -382,82 +483,6 @@
             return carry
 
         lax.fori_loop(0, chunks, one, 0)
-        if which < 2:
-            copy = pltpu.make_async_copy(gpair.at[which], gpair_hbm.at[which], store_sem.at[which])
-        else:
-            copy = pltpu.make_async_copy(gdown, gdown_hbm, store_sem.at[which])
-        copy.start()
-        return copy
-
-    own_copy.wait()
-    cross(0)
-    for k in (1, 2, 3):
-        spread(k, 0)
-    forward(0, 0)
-    relay(0, 0)
-    forward(1, 0)
-    cross(1)
-    for k in (1, 2, 3):
-        spread(k, 1)
-    forward(0, 1)
-    for k in (4, 5, 6, 7):
-        spread(k, 0)
-        spread(k, 1)
-    forward(2, 0)
-    relay(1, 0)
-    forward(1, 1)
-    relay(0, 1)
-    forward(3, 0)
-    relay(2, 0)
-    forward(2, 1)
-    relay(1, 1)
-    forward(3, 1)
-    relay(3, 0)
-    relay(2, 1)
-    loads[2].wait()
-    loads[3].wait()
-
-    def both(do, *slabs):
-        for k in slabs:
-            for h in halves:
-                do(k, h)
-
-    both(forward, 4)
-    arrived(0)
-    arrived(1)
-    compute(0, 2)
-    relay(3, 1)
-    both(relay, 4)
-    both(forward, 5)
-    both(give_on, 0, 1)
-    both(relay, 5)
-    both(forward, 6)
-    arrived(2)
-    arrived(3)
-    compute(2, 2)
-    both(settle, 0, 1)
-    both(relay, 6)
-    both(forward, 7)
-    both(give_on, 2, 3)
-    arrived(4)
-    arrived(5)
-    compute(4, 2)
-    both(settle, 2, 3)
-    both(relay, 7)
-    both(give_on, 4, 5)
-    arrived(6)
-    compute(6, 1)
-    both(settle, 4, 5)
-    arrived(7)
-    compute(7, 1)
-    both(give_on, 6)
-    both(settle, 6)
-    stores = [weight_grads(0)]
-    both(give_on, 7)
-    stores.append(weight_grads(1))
-    both(settle, 7)
-    stores.append(weight_grads(2))
-
     half = NXC * NZL * CAP
     qrow = lax.broadcasted_iota(jnp.int32, (half, half), 0)
     qcol = lax.broadcasted_iota(jnp.int32, (half, half), 1)
@@ -466,7 +491,7 @@
     wanted_back = q_off * SLAB + q_src * CAP + lax.rem(qrow, CAP)
     shuffle_back = jnp.where(qcol == wanted_back, 1.0, 0.0).astype(BF16)
 
-    def join(c, carry):
+    def add_halves(c, carry):
         parts = []
         for i in range(NZL):
             first, second = OFFSETS.index(i), OFFSETS.index(i + NZL)
@@ -479,14 +504,19 @@
 
     rx_copies = []
     own_back = []
-    for h in halves:
+
+    def join(h):
         for k in range(1, NZ):
-            rz_copies[k, h].wait_recv()
-        over(h, join)
+            for q in range(BACK_PIECES[k]):
+                if q * END_PIECES < (h + 1) * BACK_PIECES[k] and (q + 1) * END_PIECES > h * BACK_PIECES[k]:
+                    if (k, q) not in taken:
+                        rz_copies[k, q].wait_recv()
+                        taken.add((k, q))
+        over(END_PIECES, h, add_halves)
         for i in range(1, NXC):
             copy = remote(
-                xsend.at[i, :, piece(h)],
-                final.at[xc, :, piece(h)],
+                xsend.at[i, :, piece(END_PIECES, h)],
+                final.at[xc, :, piece(END_PIECES, h)],
                 rx_send.at[h, i],
                 rx_recv.at[h, i],
                 at_x(NXC - i),
@@ -494,17 +524,34 @@
             copy.start()
             rx_copies.append(copy)
         copy = pltpu.make_async_copy(
-            xsend.at[0, :, piece(h)], final.at[xc, :, piece(h)], store_sem.at[3 + h]
+            xsend.at[0, :, piece(END_PIECES, h)], final.at[xc, :, piece(END_PIECES, h)], store_sem.at[h]
         )
         copy.start()
         own_back.append(copy)
+
+    taken = set()
+    loads[2].wait()
+    loads[3].wait()
+    steps = {
+        "cross": cross,
+        "spread": spread,
+        "forward": forward,
+        "relay": relay,
+        "compute": compute,
+        "give_on": give_on,
+        "settle": settle,
+        "grads": grads,
+        "join": join,
+    }
+    for name, *where in ORDER:
+        steps[name](*where)
 
     for table in (x_copies, z_copies, y_copies, f_copies, rl_copies, ru_copies, rd_copies, rz_copies):
         for copy in table.values():
             copy.wait_send()
     for copy in rx_copies:
         copy.wait()
-    for copy in stores + own_back:
+    for copy in own_back:
         copy.wait()
 
 
@@ -523,11 +570,11 @@
         out_shape=(
             jax.ShapeDtypeStruct((NXC * NZL * CAP, tokens), BF16),
             jax.ShapeDtypeStruct((NXC, NZL * CAP, width), BF16),
-            jax.ShapeDtypeStruct((2, units, width), BF16),
-            jax.ShapeDtypeStruct((units, width), BF16),
+            pltpu.VMEM((2, units, width), BF16),
+            pltpu.VMEM((units, width), BF16),
         ),
         in_specs=[in_vmem, in_vmem, any_space, any_space, any_space, any_space],
-        out_specs=(in_vmem, any_space, any_space, any_space),
+        out_specs=(in_vmem, any_space, in_vmem, in_vmem),
         scratch_shapes=[
             vmem((tokens, width), BF16),
             vmem((tokens, width), BF16),
@@ -549,31 +596,29 @@
             vmem((NZ, SLAB, width), BF16),
             vmem((NZ, SLAB, width), BF16),
             vmem((NXC, NZL * CAP, width), BF16),
-            vmem((2, units, width), BF16),
-            vmem((units, width), BF16),
             dma((5,)),
             dma((5,)),
-            dma((HALVES, NXC)),
-            dma((HALVES, NXC)),
-            dma((HALVES, NZ)),
-            dma((HALVES, NZ)),
-            dma((2, HALVES, NZ)),
-            dma((2, HALVES, NZ)),
-            dma((HALVES, NZ)),
-            dma((HALVES, NZ)),
-            dma((HALVES, NZ)),
-            dma((HALVES, NZ)),
-            dma((HALVES, NZ)),
-            dma((HALVES, NZ)),
-            dma((HALVES, NZ)),
-            dma((HALVES, NZ)),
-            dma((HALVES, NZ)),
-            dma((HALVES, NZ)),
-            dma((HALVES, NXC)),
-            dma((HALVES, NXC)),
+            dma((X_PIECES, NXC)),
+            dma((X_PIECES, NXC)),
+            dma((MOST, NZ)),
+            dma((MOST, NZ)),
+            dma((2, MOST, NZ)),
+            dma((2, MOST, NZ)),
+            dma((MOST, NZ)),
+            dma((MOST, NZ)),
+            dma((MOST, NZ)),
+            dma((MOST, NZ)),
+            dma((MOST, NZ)),
+            dma((MOST, NZ)),
+            dma((MOST, NZ)),
+            dma((MOST, NZ)),
+            dma((MOST, NZ)),
+            dma((MOST, NZ)),
+            dma((END_PIECES, NXC)),
+            dma((END_PIECES, NXC)),
         ],
         compiler_params=pltpu.CompilerParams(
-            collective_id=0, has_side_effects=True, vmem_limit_bytes=60 * 1024 * 1024
+            collective_id=0, has_side_effects=True, vmem_limit_bytes=48 * 1024 * 1024
         ),
     )(expert_ids.reshape(1, tokens), gate_probs.reshape(1, tokens), activations, cotangent, pair, down)
     out = tn(pick, final.reshape(NXC * NZL * CAP, width)).astype(BF16)

time: 158 us -> 147 us (0.930)
  Pallas kernels: 150 us -> 140 us
    pallas_call x1, Pallas kernels: 150 us -> 140 us  [per_device(): pl.pallas_call(kernel, out_shape=(jax.ShapeDtypeStruct((NXC * NZL * CAP,...]
    unnamed x4 -> x6, local copies, waits for them, and re-layouts: 5.17 us -> 4.11 us
where the time goes in v3:
time: 147 us
  Pallas kernels  140 us (95%)
  local copies, waits for them, and re-layouts  4.11 us (3%)
    pallas_call x1, Pallas kernels, per_device(): pl.pallas_call(kernel, out_shape=(jax.ShapeDtypeStruct((NXC * NZL * CAP,...  140 us
    unnamed x6, local copies, waits for them, and re-layouts  4.11 us

profile of v3, /device:TPU:1, one launch (start us, length us, event | category | flops | bytes accessed | tf_op | source)
XLA Modules:
  0.0 146.6 jit_solution(791734802255309707)
XLA Ops:
  0.6 0.0 copy-start
  0.6 0.6 copy-done
  1.3 0.0 copy-start.1
  1.3 0.7 copy-done.1
  1.9 140.4 %shard_map.85 = (bf16[64,128]{1,0:T(8,128)(2,1)S(1)}, bf16[8,8,4096]{2,1,0:T(8,128)(2,1)S(1)}, bf16[2,192,4096]{2,1,0:T(8,128)(2,1)S(1)}, bf16[192,4096]{1,0:T(8,128)(2,1)S(1)}) custom-call(s32[1,128]{1,0:T(1,128)S(1)} %bitcast.16, f32[1,128]{1,0:T(1,128)S(1)} %bitcast.17, bf16[128,4096]{1,0:T(8,128)(2,1)} %act_hbm.1, bf16[128,4096]{1,0:T(8,128)(2,1)} %cot_hbm.1, ...), custom_call_target="tpu_custom_call" | custom-call | tf_op jit(solution)/shard_map/pallas_call | solution.py:568
  142.4 1.4 convolution_convert_fusion
  143.8 1.1 copy.12
  144.9 1.7 %copy.11 = bf16[1,2,4096,192]{2,3,1,0:T(8,128)(2,1)} copy(bf16[1,2,4096,192]{2,3,1,0:T(8,128)(2,1)S(1)} %bitcast.14) | data formatting | bytes 6291456
Async XLA Ops:
  0.6 0.7 copy-start
  1.3 0.7 copy-start.1

commit v4 on v3

--- a/solution.py
+++ b/solution.py
@@ -16,109 +16,135 @@
 NZ = NZH * NZL
 NXC = 8
 SLAB = NXC * CAP
-OFFSETS = (0, 1, 7, 2, 6, 3, 5, 4)
+OFFSETS = (0, 1, 6, 2, 4, 5, 3, 7)
 CHUNK = 512
-X_PIECES = 4
-OUT_PIECES = (4, 2, 2, 2, 2, 2, 2, 2)
-BACK_PIECES = (2, 2, 2, 2, 2, 2, 2, 2)
-END_PIECES = 2
+X_PIECES = 8
+OUT_PIECES = (4, 4, 4, 2, 2, 2, 2, 2)
+BACK_PIECES = (2, 2, 2, 2, 2, 2, 4, 4)
+END_PIECES = 4
 MOST = 4
 ORDER = (
     ('cross', 0),
+    ('cross', 1),
+    ('spread', 1, 0),
+    ('spread', 2, 0),
     ('forward', 0, 0),
-    ('cross', 1),
+    ('cross', 2),
+    ('cross', 3),
+    ('spread', 1, 1),
+    ('forward', 0, 1),
     ('spread', 3, 0),
-    ('forward', 0, 1),
-    ('spread', 2, 0),
-    ('cross', 2),
-    ('spread', 1, 0),
+    ('spread', 7, 0),
+    ('relay', 0, 0),
+    ('cross', 4),
+    ('spread', 5, 0),
+    ('cross', 5),
+    ('forward', 0, 2),
+    ('forward', 1, 0),
+    ('cross', 6),
+    ('cross', 7),
+    ('forward', 0, 3),
+    ('forward', 1, 1),
+    ('spread', 1, 3),
+    ('spread', 1, 2),
+    ('spread', 3, 1),
+    ('spread', 7, 1),
+    ('relay', 0, 2),
+    ('spread', 4, 0),
+    ('forward', 2, 0),
+    ('forward', 7, 0),
+    ('spread', 4, 1),
+    ('relay', 1, 1),
+    ('forward', 1, 3),
+    ('spread', 6, 1),
+    ('forward', 3, 0),
+    ('forward', 5, 0),
+    ('spread', 2, 2),
+    ('forward', 1, 2),
     ('spread', 6, 0),
-    ('spread', 4, 0),
-    ('spread', 5, 0),
-    ('forward', 0, 2),
-    ('relay', 0, 1),
-    ('cross', 3),
-    ('forward', 0, 3),
-    ('spread', 2, 1),
-    ('forward', 2, 0),
-    ('spread', 5, 1),
-    ('relay', 0, 0),
-    ('forward', 3, 0),
-    ('spread', 1, 1),
-    ('forward', 1, 0),
-    ('relay', 3, 0),
-    ('relay', 0, 2),
-    ('relay', 2, 0),
-    ('spread', 4, 1),
-    ('spread', 7, 0),
-    ('spread', 6, 1),
-    ('relay', 1, 0),
-    ('forward', 4, 0),
-    ('forward', 2, 1),
-    ('relay', 0, 3),
-    ('forward', 6, 0),
-    ('forward', 5, 0),
-    ('forward', 4, 1),
-    ('relay', 2, 1),
-    ('forward', 5, 1),
-    ('relay', 4, 0),
+    ('forward', 3, 1),
     ('relay', 5, 0),
-    ('spread', 7, 1),
-    ('forward', 1, 1),
-    ('relay', 5, 1),
-    ('relay', 4, 1),
-    ('forward', 7, 0),
-    ('spread', 3, 1),
-    ('relay', 1, 1),
-    ('forward', 6, 1),
-    ('relay', 6, 0),
     ('forward', 7, 1),
     ('relay', 7, 0),
+    ('spread', 2, 1),
+    ('relay', 1, 3),
+    ('relay', 2, 0),
+    ('relay', 0, 1),
+    ('relay', 3, 0),
+    ('forward', 4, 0),
+    ('spread', 5, 1),
+    ('forward', 4, 1),
+    ('relay', 4, 0),
+    ('spread', 2, 3),
+    ('forward', 2, 1),
+    ('forward', 2, 2),
+    ('relay', 4, 1),
+    ('relay', 0, 3),
+    ('forward', 5, 1),
+    ('relay', 3, 1),
+    ('forward', 6, 1),
+    ('relay', 5, 1),
+    ('forward', 2, 3),
     ('relay', 7, 1),
+    ('forward', 6, 0),
     ('relay', 6, 1),
-    ('forward', 3, 1),
+    ('relay', 2, 1),
+    ('relay', 2, 2),
+    ('relay', 2, 3),
+    ('relay', 6, 0),
     ('compute', 4, 2),
+    ('compute', 2, 2),
+    ('give_on', 5, 1),
+    ('give_on', 3, 0),
+    ('relay', 1, 0),
+    ('give_on', 5, 0),
+    ('relay', 1, 2),
+    ('give_on', 4, 0),
+    ('give_on', 4, 1),
     ('compute', 6, 2),
-    ('give_on', 4, 0),
-    ('give_on', 5, 0),
+    ('settle', 3, 0),
+    ('settle', 4, 0),
+    ('settle', 4, 1),
+    ('give_on', 6, 0),
+    ('give_on', 2, 0),
+    ('give_on', 3, 1),
+    ('settle', 5, 1),
+    ('give_on', 6, 1),
+    ('compute', 0, 2),
+    ('settle', 5, 0),
+    ('settle', 6, 0),
+    ('grads', 2),
+    ('settle', 3, 1),
     ('give_on', 7, 0),
-    ('relay', 3, 1),
-    ('give_on', 5, 1),
-    ('give_on', 6, 0),
-    ('compute', 0, 2),
-    ('give_on', 6, 1),
-    ('settle', 5, 0),
-    ('settle', 4, 0),
-    ('give_on', 4, 1),
+    ('give_on', 6, 3),
+    ('give_on', 2, 1),
+    ('give_on', 6, 2),
+    ('settle', 6, 1),
+    ('give_on', 1, 0),
     ('give_on', 7, 1),
+    ('settle', 2, 0),
+    ('give_on', 0, 0),
+    ('give_on', 0, 1),
+    ('give_on', 7, 2),
+    ('give_on', 7, 3),
+    ('settle', 6, 3),
+    ('give_on', 1, 1),
     ('settle', 7, 0),
-    ('settle', 6, 0),
-    ('compute', 2, 2),
-    ('grads', 2),
-    ('settle', 4, 1),
-    ('give_on', 0, 1),
-    ('settle', 5, 1),
-    ('give_on', 3, 0),
+    ('settle', 2, 1),
+    ('settle', 1, 0),
+    ('settle', 6, 2),
     ('settle', 7, 1),
-    ('settle', 6, 1),
-    ('give_on', 0, 0),
-    ('give_on', 1, 0),
-    ('give_on', 2, 0),
-    ('give_on', 2, 1),
-    ('give_on', 3, 1),
-    ('give_on', 1, 1),
-    ('settle', 3, 0),
-    ('settle', 1, 0),
+    ('grads', 1),
+    ('settle', 1, 1),
+    ('settle', 7, 3),
+    ('settle', 0, 0),
+    ('join', 0),
     ('settle', 0, 1),
-    ('settle', 2, 0),
-    ('settle', 0, 0),
-    ('settle', 3, 1),
-    ('settle', 1, 1),
-    ('settle', 2, 1),
-    ('join', 0),
+    ('settle', 7, 2),
+    ('join', 1),
+    ('join', 3),
+    ('join', 2),
     ('grads', 0),
-    ('join', 1),
-    ('grads', 1),
 )
 
 
@@ -135,8 +161,8 @@
 
 
 def kernel(
-    ids_ref,
-    probs_ref,
+    ids_hbm,
+    probs_hbm,
     act_hbm,
     cot_hbm,
     pair_hbm,
@@ -145,6 +171,8 @@
     final,
     gpair,
     gdown,
+    ids_ref,
+    probs_ref,
     act,
     cot,
     pair,
@@ -228,6 +256,12 @@
         pltpu.make_async_copy(pair_hbm, pair, load_sem.at[2]),
         pltpu.make_async_copy(down_hbm, down, load_sem.at[3]),
     ]
+    small_loads = [
+        pltpu.make_async_copy(ids_hbm, ids_ref, load_sem.at[5]),
+        pltpu.make_async_copy(probs_hbm, probs_ref, load_sem.at[6]),
+    ]
+    for copy in small_loads:
+        copy.start()
     for copy in loads:
         copy.start()
     barrier = pltpu.get_barrier_semaphore()
@@ -236,6 +270,8 @@
     for partner in partners:
         pl.semaphore_signal(barrier, inc=1, device_id=partner, device_id_type=MESH)
 
+    for copy in small_loads:
+        copy.wait()
     ids = ids_ref[...]
     ids_wide = jnp.broadcast_to(ids.astype(F32), (tokens, tokens))
     ids_tall = ids_wide.T
@@ -563,6 +599,7 @@
     dma = pltpu.SemaphoreType.DMA
     vmem = pltpu.VMEM
     any_space = pl.BlockSpec(memory_space=pl.ANY)
+    in_hbm = pl.BlockSpec(memory_space=pltpu.HBM)
     in_vmem = pl.BlockSpec(memory_space=pltpu.VMEM)
     total_rows = NZ * NY * SLAB
     pick, final, gpair, gdown = pl.pallas_call(
@@ -573,9 +610,11 @@
             pltpu.VMEM((2, units, width), BF16),
             pltpu.VMEM((units, width), BF16),
         ),
-        in_specs=[in_vmem, in_vmem, any_space, any_space, any_space, any_space],
+        in_specs=[in_hbm, in_hbm, in_hbm, in_hbm, in_hbm, in_hbm],
         out_specs=(in_vmem, any_space, in_vmem, in_vmem),
         scratch_shapes=[
+            vmem((1, tokens), jnp.int32),
+            vmem((1, tokens), F32),
             vmem((tokens, width), BF16),
             vmem((tokens, width), BF16),
             vmem((2, units, width), BF16),
@@ -596,7 +635,7 @@
             vmem((NZ, SLAB, width), BF16),
             vmem((NZ, SLAB, width), BF16),
             vmem((NXC, NZL * CAP, width), BF16),
-            dma((5,)),
+            dma((7,)),
             dma((5,)),
             dma((X_PIECES, NXC)),
             dma((X_PIECES, NXC)),

time: 147 us -> 144 us (0.980)
  Pallas kernels: 140 us -> 138 us
    pallas_call x1, Pallas kernels: 140 us -> 138 us  [per_device(): pl.pallas_call(kernel, out_shape=(jax.ShapeDtypeStruct((NXC * NZL * CAP,...]
where the time goes in v4:
time: 144 us
  Pallas kernels  138 us (96%)
  local copies, waits for them, and re-layouts  4.11 us (3%)
  matrix products  1.44 us (1%)
    pallas_call x1, Pallas kernels, per_device(): pl.pallas_call(kernel, out_shape=(jax.ShapeDtypeStruct((NXC * NZL * CAP,...  138 us
    unnamed x6, local copies, waits for them, and re-layouts  4.11 us

profile of v4, /device:TPU:1, one launch (start us, length us, event | category | flops | bytes accessed | tf_op | source)
XLA Modules:
  0.0 144.3 jit_solution(14513520641948123983)
XLA Ops:
  0.6 0.0 copy-start
  0.6 0.6 copy-done
  1.3 0.0 copy-start.1
  1.3 0.7 copy-done.1
  1.9 138.1 %shard_map.85 = (bf16[64,128]{1,0:T(8,128)(2,1)S(1)}, bf16[8,8,4096]{2,1,0:T(8,128)(2,1)S(1)}, bf16[2,192,4096]{2,1,0:T(8,128)(2,1)S(1)}, bf16[192,4096]{1,0:T(8,128)(2,1)S(1)}) custom-call(s32[1,128]{1,0:T(1,128)S(1)} %bitcast.16, f32[1,128]{1,0:T(1,128)S(1)} %bitcast.17, bf16[128,4096]{1,0:T(8,128)(2,1)} %act_hbm.1, bf16[128,4096]{1,0:T(8,128)(2,1)} %cot_hbm.1, ...), custom_call_target="tpu_custom_call" | custom-call | tf_op jit(solution)/shard_map/pallas_call | solution.py:605
  140.1 1.4 convolution_convert_fusion
  141.5 1.1 copy.12
  142.7 1.7 %copy.11 = bf16[1,2,4096,192]{2,3,1,0:T(8,128)(2,1)} copy(bf16[1,2,4096,192]{2,3,1,0:T(8,128)(2,1)S(1)} %bitcast.14) | data formatting | bytes 6291456
Async XLA Ops:
  0.6 0.7 copy-start
  1.3 0.7 copy-start.1
